TPU v7x, 32 devices: a whole 2x2x4 slice. The times are simulated.
32 devices in a mesh: row: 8 (over z, core), col: 4 (over y, x).
Axes of the slice: x: 2, y: 2, z: 4, core: 2. Of those that a mesh axis runs over, the one named last changes fastest.
Arguments:
- amplitudes: float32 [8, 4, 2, 65536], P('row', 'col'), may hold values from -6 to 6
- gate_real: float32 [2, 3, 128, 128], replicated, may hold values from -0.375 to 0.375
- gate_imag: float32 [2, 3, 128, 128], replicated, may hold values from -0.375 to 0.375
- gate_qubits: int32 [2, 3, 9], replicated, may hold values from 0 to 8, each once within a row
- swap_qubits: int32 [2, 9], replicated, may hold values from 0 to 8, each once within a row
Outputs:
- evolved: float32 [8, 4, 2, 65536], P('row', 'col')
Inputs may be any that keep to these rules, and one draw needn't show every extreme that they name: `gate_qubits`: each row is an ordering of 0 to 8; a gate acts on local qubits 7 + its first 7 entries, entry j giving bit j of the gate index. `swap_qubits`: each row is an ordering of 0 to 8; in a round on an axis with k index bits, local qubit 7 + entry j for j < k is swapped with bit j of that axis's index.
All inputs are finite; a program needn't handle non-finite values.
Results may differ from a plain program's by a relative error of at most 0.0001.
Values sent between devices are 32-bit elements; how exact they have to be, the bound alone decides.
No kernel may reach another device: no remote copies, remote signals or barrier semaphores. Data moves between devices by JAX's collectives and lax.ppermute only.
A program may use at most 64 MiB of HBM per device.

v0:
```python
import jax
import jax.numpy as jnp
from jax import lax
from jax.sharding import PartitionSpec as P


def spread_bits(dest, total_bits):
    low_count = total_bits // 2
    high_count = total_bits - low_count

    def table(count, offset):
        position = jnp.arange(2**count, dtype=jnp.int32)
        result = jnp.zeros_like(position)
        for bit_index in range(count):
            result = result + jnp.left_shift(position >> bit_index & 1, dest[offset + bit_index])
        return result

    low_table = table(low_count, 0)
    high_table = table(high_count, low_count)
    return (high_table[:, None] + low_table[None, :]).reshape(-1)


def qubit_maps(chosen, top_count, total_bits):
    qubits = jnp.arange(total_bits, dtype=jnp.int32)
    picked = chosen[:top_count]
    matches = picked[:, None] == qubits[None, :]
    chosen_mask = jnp.any(matches, axis=0)
    slot_top = jnp.sum(
        jnp.where(matches, jnp.arange(top_count, dtype=jnp.int32)[:, None], 0), axis=0
    )
    unchosen = jnp.where(chosen_mask, 0, 1).astype(jnp.int32)
    rest_rank = jnp.cumsum(unchosen) - unchosen
    ordering = jnp.argsort(jnp.where(chosen_mask, total_bits + qubits, qubits))
    low_bits = total_bits - top_count
    forward_dest = jnp.concatenate([ordering[:low_bits], picked])
    backward_dest = jnp.where(chosen_mask, low_bits + slot_top, rest_rank)
    return (spread_bits(forward_dest, total_bits), spread_bits(backward_dest, total_bits))


def per_device(amplitudes, gate_real, gate_imag, gate_qubits, swap_qubits):
    local_size = amplitudes.shape[-1]
    total_bits = local_size.bit_length() - 1
    gate_size = gate_real.shape[-1]
    gate_bits = gate_size.bit_length() - 1
    high_bits = total_bits - gate_bits
    row_count = local_size // gate_size
    current = amplitudes.reshape(2, row_count, gate_size)
    for round_index in range(gate_real.shape[0]):
        for gate_index in range(gate_real.shape[1]):
            forward, backward = qubit_maps(
                gate_qubits[round_index, gate_index], gate_bits, high_bits
            )
            gathered = jnp.take(current, forward, axis=1, mode="clip").reshape(
                2 * gate_size, local_size // gate_size
            )
            real_part = gate_real[round_index, gate_index]
            imag_part = gate_imag[round_index, gate_index]
            operator = jnp.concatenate(
                [
                    jnp.concatenate([real_part, -imag_part], 1),
                    jnp.concatenate([imag_part, real_part], 1),
                ],
                0,
            )
            applied = jnp.dot(
                operator,
                gathered,
                precision=lax.Precision.HIGHEST,
                preferred_element_type=jnp.float32,
            ).reshape(2, row_count, gate_size)
            current = jnp.take(applied, backward, axis=1, mode="clip")
            current = (
                current.reshape(2, row_count // gate_size, gate_size, gate_size)
                .transpose(0, 1, 3, 2)
                .reshape(2, row_count, gate_size)
            )
        if round_index % 2 == 0:
            devices = lax.axis_size("row")
            forward, backward = qubit_maps(
                swap_qubits[round_index], devices.bit_length() - 1, high_bits
            )
            prepared = jnp.take(current, forward, axis=1, mode="clip").reshape(
                2, devices, local_size // devices
            )
            arrived = lax.all_to_all(prepared, "row", split_axis=1, concat_axis=1, tiled=True)
        else:
            devices = lax.axis_size("col")
            forward, backward = qubit_maps(
                swap_qubits[round_index], devices.bit_length() - 1, high_bits
            )
            prepared = jnp.take(current, forward, axis=1, mode="clip").reshape(
                2, devices, local_size // devices
            )
            arrived = lax.all_to_all(prepared, "col", split_axis=1, concat_axis=1, tiled=True)
        current = jnp.take(arrived.reshape(2, row_count, gate_size), backward, axis=1, mode="clip")
    return current.reshape(amplitudes.shape)


def solution(mesh):
    placed = (P("row", "col", None, None), P(), P(), P(), P())
    return jax.shard_map(
        per_device,
        mesh=mesh,
        in_specs=placed,
        out_specs=P("row", "col", None, None),
        check_vma=False,
    )
```

profile of v0, /device:TPU:0, one launch (start us, length us, event | category | flops | bytes accessed | tf_op | source)
XLA Modules:
  0.0 183.7 jit_solution(13351006384527950985)
XLA Ops:
  8.8 3.2 %shift-left_add_fusion.31 = s32[32]{0:T(128)S(1)} fusion(s32[]{:T(128)} %bitcast.17, s32[]{:T(128)} %bitcast.16, s32[]{:T(128)} %bitcast.15, s32[]{:T(128)} %bitcast.14, s32[]{:T(128)} %bitcast.13), kind=kLoop, calls=%fused_computation.200 | loop fusion | flops 608 | bytes 148 | tf_op jit(solution)/shard_map/add | solution.py:15
  20.5 3.3 %shift-left_add_fusion.29 = s32[32]{0:T(128)S(1)} fusion(s32[]{:T(128)} %bitcast.30, s32[]{:T(128)} %bitcast.29, s32[]{:T(128)} %bitcast.28, s32[]{:T(128)} %bitcast.27, s32[]{:T(128)} %bitcast.26), kind=kLoop, calls=%fused_computation.191 | loop fusion | flops 608 | bytes 148 | tf_op jit(solution)/shard_map/add | solution.py:15
  31.3 3.1 %shift-left_add_fusion.27 = s32[32]{0:T(128)S(1)} fusion(s32[]{:T(128)} %bitcast.43, s32[]{:T(128)} %bitcast.42, s32[]{:T(128)} %bitcast.41, s32[]{:T(128)} %bitcast.40, s32[]{:T(128)} %bitcast.39), kind=kLoop, calls=%fused_computation.189 | loop fusion | flops 608 | bytes 148 | tf_op jit(solution)/shard_map/add | solution.py:15
  41.0 3.1 %shift-left_add_fusion.25 = s32[32]{0:T(128)S(1)} fusion(s32[]{:T(128)} %bitcast.56, s32[]{:T(128)} %bitcast.55, s32[]{:T(128)} %bitcast.54, s32[]{:T(128)} %bitcast.53, s32[]{:T(128)} %bitcast.52), kind=kLoop, calls=%fused_computation.185 | loop fusion | flops 608 | bytes 148 | tf_op jit(solution)/shard_map/add | solution.py:15
  51.5 3.2 %shift-left_add_fusion.23 = s32[32]{0:T(128)S(1)} fusion(s32[]{:T(128)} %bitcast.69, s32[]{:T(128)} %bitcast.68, s32[]{:T(128)} %bitcast.67, s32[]{:T(128)} %bitcast.66, s32[]{:T(128)} %bitcast.65), kind=kLoop, calls=%fused_computation.183 | loop fusion | flops 608 | bytes 148 | tf_op jit(solution)/shard_map/add | solution.py:15
  58.8 2.6 %shift-left_add_fusion.20 = s32[16]{0:T(128)S(1)} fusion(s32[]{:T(128)} %bitcast.86, s32[]{:T(128)} %bitcast.85, s32[]{:T(128)} %bitcast.84, s32[]{:T(128)} %bitcast.83), kind=kLoop, calls=%fused_computation.178 | loop fusion | flops 240 | bytes 80 | tf_op jit(solution)/shard_map/add | solution.py:15
  61.4 3.1 %shift-left_add_fusion.21 = s32[32]{0:T(128)S(1)} fusion(s32[]{:T(128)} %bitcast.82, s32[]{:T(128)} %bitcast.81, s32[]{:T(128)} %bitcast.80, s32[]{:T(128)} %bitcast.79, s32[]{:T(128)} %bitcast.78), kind=kLoop, calls=%fused_computation.179 | loop fusion | flops 608 | bytes 148 | tf_op jit(solution)/shard_map/add | solution.py:15
  72.0 3.1 %shift-left_add_fusion.19 = s32[32]{0:T(128)S(1)} fusion(s32[]{:T(128)} %bitcast.96, s32[]{:T(128)} %bitcast.95, s32[]{:T(128)} %bitcast.94, s32[]{:T(128)} %bitcast.93, s32[]{:T(128)} %bitcast.92), kind=kLoop, calls=%fused_computation.175 | loop fusion | flops 608 | bytes 148 | tf_op jit(solution)/shard_map/add | solution.py:15
  75.3 2.5 %gather_fusion.6 = f32[512,2,128]{2,1,0:T(2,128)} fusion(f32[2,512,128]{2,0,1:T(2,128)S(1)} %copy.95, s32[1024]{0:T(1024)S(1)} %pad_clamp_fusion.9), kind=kCustom, calls=%fused_computation.6 | custom fusion | bytes 1050624 | tf_op jit(solution)/shard_map/jit(_take)/gather | solution.py:82
  77.9 6.4 %all-to-all-start = ((f32[2,8,8192]{2,0,1:T(2,128)}), f32[2,8,8192]{2,0,1:T(2,128)S(1)}, u32[]{:S(2)}, u32[]{:S(2)}) async-start(f32[2,8,8192]{2,0,1:T(2,128)} %bitcast.102), calls=%async_computation | async-start | bytes 1048576 | tf_op jit(solution)/shard_map/all_to_all | solution.py:85
  99.8 3.1 %shift-left_add_fusion.17 = s32[32]{0:T(128)S(1)} fusion(s32[]{:T(128)} %bitcast.110, s32[]{:T(128)} %bitcast.109, s32[]{:T(128)} %bitcast.108, s32[]{:T(128)} %bitcast.107, s32[]{:T(128)} %bitcast.106), kind=kLoop, calls=%fused_computation.173 | loop fusion | flops 608 | bytes 148 | tf_op jit(solution)/shard_map/add | solution.py:15
  105.4 3.2 %shift-left_add_fusion.15 = s32[32]{0:T(128)S(1)} fusion(s32[]{:T(128)} %bitcast.120, s32[]{:T(128)} %bitcast.119, s32[]{:T(128)} %bitcast.118, s32[]{:T(128)} %bitcast.117, s32[]{:T(128)} %bitcast.116), kind=kLoop, calls=%fused_computation.171 | loop fusion | flops 608 | bytes 148 | tf_op jit(solution)/shard_map/add | solution.py:15
  111.2 3.2 %shift-left_add_fusion.13 = s32[32]{0:T(128)S(1)} fusion(s32[]{:T(128)} %bitcast.133, s32[]{:T(128)} %bitcast.132, s32[]{:T(128)} %bitcast.131, s32[]{:T(128)} %bitcast.130, s32[]{:T(128)} %bitcast.129), kind=kLoop, calls=%fused_computation.167 | loop fusion | flops 608 | bytes 148 | tf_op jit(solution)/shard_map/add | solution.py:15
  116.8 3.2 %shift-left_add_fusion.11 = s32[32]{0:T(128)S(1)} fusion(s32[]{:T(128)} %bitcast.146, s32[]{:T(128)} %bitcast.145, s32[]{:T(128)} %bitcast.144, s32[]{:T(128)} %bitcast.143, s32[]{:T(128)} %bitcast.142), kind=kLoop, calls=%fused_computation.165 | loop fusion | flops 608 | bytes 148 | tf_op jit(solution)/shard_map/add | solution.py:15
  122.6 3.1 %shift-left_add_fusion.9 = s32[32]{0:T(128)S(1)} fusion(s32[]{:T(128)} %bitcast.159, s32[]{:T(128)} %bitcast.158, s32[]{:T(128)} %bitcast.157, s32[]{:T(128)} %bitcast.156, s32[]{:T(128)} %bitcast.155), kind=kLoop, calls=%fused_computation.161 | loop fusion | flops 608 | bytes 148 | tf_op jit(solution)/shard_map/add | solution.py:15
  125.7 2.6 %shift-left_add_fusion.6 = s32[16]{0:T(128)S(1)} fusion(s32[]{:T(128)} %bitcast.177, s32[]{:T(128)} %bitcast.176, s32[]{:T(128)} %bitcast.175, s32[]{:T(128)} %bitcast.174), kind=kLoop, calls=%fused_computation.156 | loop fusion | flops 240 | bytes 80 | tf_op jit(solution)/shard_map/add | solution.py:15
  128.3 3.0 %shift-left_add_fusion.7 = s32[32]{0:T(128)S(1)} fusion(s32[]{:T(128)} %bitcast.172, s32[]{:T(128)} %bitcast.171, s32[]{:T(128)} %bitcast.170, s32[]{:T(128)} %bitcast.169, s32[]{:T(128)} %bitcast.168), kind=kLoop, calls=%fused_computation.159 | loop fusion | flops 608 | bytes 148 | tf_op jit(solution)/shard_map/add | solution.py:15
  133.9 3.2 %shift-left_add_fusion.5 = s32[32]{0:T(128)S(1)} fusion(s32[]{:T(128)} %bitcast.185, s32[]{:T(128)} %bitcast.184, s32[]{:T(128)} %bitcast.183, s32[]{:T(128)} %bitcast.182, s32[]{:T(128)} %bitcast.181), kind=kLoop, calls=%fused_computation.155 | loop fusion | flops 608 | bytes 148 | tf_op jit(solution)/shard_map/add | solution.py:15
  139.7 3.1 %shift-left_add_fusion.3 = s32[32]{0:T(128)S(1)} fusion(s32[]{:T(128)} %bitcast.199, s32[]{:T(128)} %bitcast.198, s32[]{:T(128)} %bitcast.197, s32[]{:T(128)} %bitcast.196, s32[]{:T(128)} %bitcast.195), kind=kLoop, calls=%fused_computation.151 | loop fusion | flops 608 | bytes 148 | tf_op jit(solution)/shard_map/add | solution.py:15
  166.3 2.5 %gather_fusion.14 = f32[512,2,128]{2,1,0:T(2,128)} fusion(f32[2,512,128]{2,0,1:T(2,128)S(1)} %copy.111, s32[1024]{0:T(1024)S(1)} %pad_clamp_fusion.1), kind=kCustom, calls=%fused_computation.14 | custom fusion | bytes 1050624 | tf_op jit(solution)/shard_map/jit(_take)/gather | solution.py:91
  168.8 3.7 %all-to-all-start.1 = ((f32[2,4,16384]{2,0,1:T(2,128)}), f32[2,4,16384]{2,0,1:T(2,128)S(1)}, u32[]{:S(2)}, u32[]{:S(2)}) async-start(f32[2,4,16384]{2,0,1:T(2,128)} %bitcast.205), calls=%async_computation.1 | async-start | bytes 1048576 | tf_op jit(solution)/shard_map/all_to_all | solution.py:94
  172.5 3.1 %shift-left_add_fusion.1 = s32[32]{0:T(128)S(1)} fusion(s32[]{:T(128)} %bitcast.213, s32[]{:T(128)} %bitcast.212, s32[]{:T(128)} %bitcast.211, s32[]{:T(128)} %bitcast.210, s32[]{:T(128)} %bitcast.209), kind=kLoop, calls=%fused_computation.149 | loop fusion | flops 608 | bytes 148 | tf_op jit(solution)/shard_map/add | solution.py:15
  175.7 5.5 %all-to-all-done.1 = f32[2,4,16384]{2,0,1:T(2,128)S(1)} async-done(((f32[2,4,16384]{2,0,1:T(2,128)}), f32[2,4,16384]{2,0,1:T(2,128)S(1)}, u32[]{:S(2)}, u32[]{:S(2)}) %all-to-all-start.1) | async-done | bytes 524320 | tf_op jit(solution)/shard_map/all_to_all | solution.py:94
  181.2 2.5 %gather_fusion.15 = f32[512,2,128]{2,1,0:T(2,128)} fusion(f32[2,512,128]{2,0,1:T(2,128)S(1)} %bitcast.307, s32[1024]{0:T(1024)S(1)} %pad_clamp_fusion), kind=kCustom, calls=%fused_computation.15 | custom fusion | bytes 1050624 | tf_op jit(solution)/shard_map/jit(_take)/gather | solution.py:95
  (203 shorter events, 104.4 us)
Async XLA Ops:
  0.0 12.1 %copy-start = (f32[1,1,2,65536]{3,2,1,0:T(2,128)S(1)}, f32[1,1,2,65536]{3,2,1,0:T(2,128)}, u32[]{:S(2)}) copy-start(f32[1,1,2,65536]{3,2,1,0:T(2,128)} %param.5) | copy-start | bytes 1572868
  0.0 1.7 copy-start.3
  2.7 0.7 copy-start.4
  14.3 1.0 copy-start.1
  15.3 1.0 copy-start.2
  77.9 68.3 %all-to-all-start = ((f32[2,8,8192]{2,0,1:T(2,128)}), f32[2,8,8192]{2,0,1:T(2,128)S(1)}, u32[]{:S(2)}, u32[]{:S(2)}) async-start(f32[2,8,8192]{2,0,1:T(2,128)} %bitcast.102), calls=%async_computation | async-start | bytes 1048576 | tf_op jit(solution)/shard_map/all_to_all | solution.py:85
  168.8 12.4 %all-to-all-start.1 = ((f32[2,4,16384]{2,0,1:T(2,128)}), f32[2,4,16384]{2,0,1:T(2,128)S(1)}, u32[]{:S(2)}, u32[]{:S(2)}) async-start(f32[2,4,16384]{2,0,1:T(2,128)} %bitcast.205), calls=%async_computation.1 | async-start | bytes 1048576 | tf_op jit(solution)/shard_map/all_to_all | solution.py:94
where the time goes:
time: 185 us; the launch traced here: 184 us
  other arithmetic  104 us (56%)
  local copies, waits for them, and re-layouts  59.7 us (32%)
  starting transfers between devices  10.1 us (5%)
  waiting for transfers between devices  5.47 us (3%)
  matrix products  3.62 us (2%)
    add x32, other arithmetic, table(): result + jnp.left_shift(position >> bit_index & 1, dest[offset + bit_index])  90 us
    gather x14, local copies, waits for them, and re-layouts, per_device(): jnp.take(current, forward, axis=1, mode='clip')  17.7 us
    slice x20, local copies, waits for them, and re-layouts, table(): dest[offset + bit_index]  14.3 us
    gather x6, local copies, waits for them, and re-layouts, per_device(): current = jnp.take(applied, backward, axis=1, mode='clip')  12.5 us
    sort x8, other arithmetic, qubit_maps(): ordering = jnp.argsort(jnp.where(chosen_mask, total_bits + qubits, qubits))  10.3 us
    all_to_all x1, starting transfers between devices, per_device(): lax.all_to_all(prepared, 'row', split_axis=1, concat_axis=1, tiled=True)  6.36 us
    all_to_all x1, waiting for transfers between devices, per_device(): lax.all_to_all(prepared, 'col', split_axis=1, concat_axis=1, tiled=True)  5.47 us
    gather x2, local copies, waits for them, and re-layouts, per_device(): jnp.take(arrived.reshape(2, row_count, gate_size), backward, axis=1, mode...  4.6 us
  transfers between devices with their start and end apart: 2, of which 1 were waited for; matrix products, arithmetic and copies ran while one was open for 35% of the time, Pallas kernels for 0%

commit v1 on v0

--- a/solution.py
+++ b/solution.py
@@ -2,6 +2,15 @@
 import jax.numpy as jnp
 from jax import lax
 from jax.sharding import PartitionSpec as P
+
+
+def orders_try_all(x_in):
+    return jnp.concatenate(
+        jax.lax.all_to_all(
+            jnp.stack(jnp.split(x_in, jax.lax.axis_size("row"), axis=1)), "row", 0, 0
+        ),
+        axis=1,
+    )
 
 
 def spread_bits(dest, total_bits):
@@ -82,7 +91,7 @@
             prepared = jnp.take(current, forward, axis=1, mode="clip").reshape(
                 2, devices, local_size // devices
             )
-            arrived = lax.all_to_all(prepared, "row", split_axis=1, concat_axis=1, tiled=True)
+            arrived = orders_try_all(prepared)
         else:
             devices = lax.axis_size("col")
             forward, backward = qubit_maps(

time: 185 us -> 192 us (1.038)
  local copies, waits for them, and re-layouts: 59.7 us -> 66.1 us
    unnamed x10 -> x17, local copies, waits for them, and re-layouts: 2.46 us -> 7.24 us
    gather x14 -> x15, local copies, waits for them, and re-layouts: 17.7 us -> 17.5 us  [per_device(): jnp.take(current, forward, axis=1, mode='clip')]
  transfers between devices with their start and end apart: 2 -> 2, of which waited for: 1 -> 1; matrix products, arithmetic and copies ran while one was open for 35% -> 34% of each run, Pallas kernels for 0% -> 0%
where the time goes in v1:
time: 192 us; the launch traced here: 190 us
  other arithmetic  104 us (54%)
  local copies, waits for them, and re-layouts  66.1 us (34%)
  starting transfers between devices  10.1 us (5%)
  waiting for transfers between devices  5.42 us (3%)
  matrix products  3.62 us (2%)
    add x32, other arithmetic, table(): result + jnp.left_shift(position >> bit_index & 1, dest[offset + bit_index])  90 us
    gather x15, local copies, waits for them, and re-layouts, per_device(): jnp.take(current, forward, axis=1, mode='clip')  17.5 us
    slice x20, local copies, waits for them, and re-layouts, table(): dest[offset + bit_index]  14.3 us
    gather x6, local copies, waits for them, and re-layouts, per_device(): current = jnp.take(applied, backward, axis=1, mode='clip')  12.7 us
    sort x8, other arithmetic, qubit_maps(): ordering = jnp.argsort(jnp.where(chosen_mask, total_bits + qubits, qubits))  10.3 us
    unnamed x17, local copies, waits for them, and re-layouts  7.24 us
    all_to_all x1, starting transfers between devices, orders_try_all(): jax.lax.all_to_all(jnp.stack(jnp.split(x_in, jax.lax.axis_size('row'), ax...  6.35 us
    all_to_all x1, waiting for transfers between devices, per_device(): lax.all_to_all(prepared, 'col', split_axis=1, concat_axis=1, tiled=True)  5.42 us
  transfers between devices with their start and end apart: 2, of which 1 were waited for; matrix products, arithmetic and copies ran while one was open for 34% of the time, Pallas kernels for 0%

profile of v1, /device:TPU:0, one launch (start us, length us, event | category | flops | bytes accessed | tf_op | source)
XLA Modules:
  0.0 190.1 jit_solution(3352906829755794238)
XLA Ops:
  8.8 3.2 %shift-left_add_fusion.31 = s32[32]{0:T(128)S(1)} fusion(s32[]{:T(128)} %bitcast.17, s32[]{:T(128)} %bitcast.16, s32[]{:T(128)} %bitcast.15, s32[]{:T(128)} %bitcast.14, s32[]{:T(128)} %bitcast.13), kind=kLoop, calls=%fused_computation.216 | loop fusion | flops 608 | bytes 148 | tf_op jit(solution)/shard_map/add | solution.py:24
  20.6 3.3 %shift-left_add_fusion.29 = s32[32]{0:T(128)S(1)} fusion(s32[]{:T(128)} %bitcast.30, s32[]{:T(128)} %bitcast.29, s32[]{:T(128)} %bitcast.28, s32[]{:T(128)} %bitcast.27, s32[]{:T(128)} %bitcast.26), kind=kLoop, calls=%fused_computation.207 | loop fusion | flops 608 | bytes 148 | tf_op jit(solution)/shard_map/add | solution.py:24
  31.3 3.1 %shift-left_add_fusion.27 = s32[32]{0:T(128)S(1)} fusion(s32[]{:T(128)} %bitcast.43, s32[]{:T(128)} %bitcast.42, s32[]{:T(128)} %bitcast.41, s32[]{:T(128)} %bitcast.40, s32[]{:T(128)} %bitcast.39), kind=kLoop, calls=%fused_computation.205 | loop fusion | flops 608 | bytes 148 | tf_op jit(solution)/shard_map/add | solution.py:24
  41.0 3.1 %shift-left_add_fusion.25 = s32[32]{0:T(128)S(1)} fusion(s32[]{:T(128)} %bitcast.56, s32[]{:T(128)} %bitcast.55, s32[]{:T(128)} %bitcast.54, s32[]{:T(128)} %bitcast.53, s32[]{:T(128)} %bitcast.52), kind=kLoop, calls=%fused_computation.201 | loop fusion | flops 608 | bytes 148 | tf_op jit(solution)/shard_map/add | solution.py:24
  51.5 3.2 %shift-left_add_fusion.23 = s32[32]{0:T(128)S(1)} fusion(s32[]{:T(128)} %bitcast.69, s32[]{:T(128)} %bitcast.68, s32[]{:T(128)} %bitcast.67, s32[]{:T(128)} %bitcast.66, s32[]{:T(128)} %bitcast.65), kind=kLoop, calls=%fused_computation.199 | loop fusion | flops 608 | bytes 148 | tf_op jit(solution)/shard_map/add | solution.py:24
  58.9 2.6 %shift-left_add_fusion.20 = s32[16]{0:T(128)S(1)} fusion(s32[]{:T(128)} %bitcast.86, s32[]{:T(128)} %bitcast.85, s32[]{:T(128)} %bitcast.84, s32[]{:T(128)} %bitcast.83), kind=kLoop, calls=%fused_computation.194 | loop fusion | flops 240 | bytes 80 | tf_op jit(solution)/shard_map/add | solution.py:24
  61.4 3.1 %shift-left_add_fusion.21 = s32[32]{0:T(128)S(1)} fusion(s32[]{:T(128)} %bitcast.82, s32[]{:T(128)} %bitcast.81, s32[]{:T(128)} %bitcast.80, s32[]{:T(128)} %bitcast.79, s32[]{:T(128)} %bitcast.78), kind=kLoop, calls=%fused_computation.195 | loop fusion | flops 608 | bytes 148 | tf_op jit(solution)/shard_map/add | solution.py:24
  72.1 3.1 %shift-left_add_fusion.19 = s32[32]{0:T(128)S(1)} fusion(s32[]{:T(128)} %bitcast.96, s32[]{:T(128)} %bitcast.95, s32[]{:T(128)} %bitcast.94, s32[]{:T(128)} %bitcast.93, s32[]{:T(128)} %bitcast.92), kind=kLoop, calls=%fused_computation.191 | loop fusion | flops 608 | bytes 148 | tf_op jit(solution)/shard_map/add | solution.py:24
  83.3 6.4 %all-to-all-start = ((f32[8,2,1,8192]{3,2,1,0:T(1,128)}), f32[8,2,1,8192]{3,2,1,0:T(1,128)S(1)}, u32[]{:S(2)}, u32[]{:S(2)}) async-start(f32[8,2,1,8192]{3,2,1,0:T(1,128)} %fusion.48), calls=%async_computation | async-start | bytes 1048576 | tf_op jit(solution)/shard_map/all_to_all | solution.py:9
  102.0 2.5 %shift-left_add_fusion.2 = s32[16]{0:T(128)S(1)} fusion(s32[]{:T(128)} %bitcast.210, s32[]{:T(128)} %bitcast.209, s32[]{:T(128)} %bitcast.208, s32[]{:T(128)} %bitcast.207), kind=kLoop, calls=%fused_computation.166 | loop fusion | flops 240 | bytes 80 | tf_op jit(solution)/shard_map/add | solution.py:24
  104.5 3.1 %shift-left_add_fusion.3 = s32[32]{0:T(128)S(1)} fusion(s32[]{:T(128)} %bitcast.206, s32[]{:T(128)} %bitcast.205, s32[]{:T(128)} %bitcast.204, s32[]{:T(128)} %bitcast.203, s32[]{:T(128)} %bitcast.202), kind=kLoop, calls=%fused_computation.167 | loop fusion | flops 608 | bytes 148 | tf_op jit(solution)/shard_map/add | solution.py:24
  110.1 3.2 %shift-left_add_fusion.17 = s32[32]{0:T(128)S(1)} fusion(s32[]{:T(128)} %bitcast.117, s32[]{:T(128)} %bitcast.116, s32[]{:T(128)} %bitcast.115, s32[]{:T(128)} %bitcast.114, s32[]{:T(128)} %bitcast.113), kind=kLoop, calls=%fused_computation.189 | loop fusion | flops 608 | bytes 148 | tf_op jit(solution)/shard_map/add | solution.py:24
  115.9 3.2 %shift-left_add_fusion.15 = s32[32]{0:T(128)S(1)} fusion(s32[]{:T(128)} %bitcast.127, s32[]{:T(128)} %bitcast.126, s32[]{:T(128)} %bitcast.125, s32[]{:T(128)} %bitcast.124, s32[]{:T(128)} %bitcast.123), kind=kLoop, calls=%fused_computation.187 | loop fusion | flops 608 | bytes 148 | tf_op jit(solution)/shard_map/add | solution.py:24
  121.6 3.0 %shift-left_add_fusion.13 = s32[32]{0:T(128)S(1)} fusion(s32[]{:T(128)} %bitcast.140, s32[]{:T(128)} %bitcast.139, s32[]{:T(128)} %bitcast.138, s32[]{:T(128)} %bitcast.137, s32[]{:T(128)} %bitcast.136), kind=kLoop, calls=%fused_computation.183 | loop fusion | flops 608 | bytes 148 | tf_op jit(solution)/shard_map/add | solution.py:24
  127.1 3.2 %shift-left_add_fusion.11 = s32[32]{0:T(128)S(1)} fusion(s32[]{:T(128)} %bitcast.153, s32[]{:T(128)} %bitcast.152, s32[]{:T(128)} %bitcast.151, s32[]{:T(128)} %bitcast.150, s32[]{:T(128)} %bitcast.149), kind=kLoop, calls=%fused_computation.181 | loop fusion | flops 608 | bytes 148 | tf_op jit(solution)/shard_map/add | solution.py:24
  132.8 3.2 %shift-left_add_fusion.9 = s32[32]{0:T(128)S(1)} fusion(s32[]{:T(128)} %bitcast.166, s32[]{:T(128)} %bitcast.165, s32[]{:T(128)} %bitcast.164, s32[]{:T(128)} %bitcast.163, s32[]{:T(128)} %bitcast.162), kind=kLoop, calls=%fused_computation.177 | loop fusion | flops 608 | bytes 148 | tf_op jit(solution)/shard_map/add | solution.py:24
  138.6 3.0 %shift-left_add_fusion.7 = s32[32]{0:T(128)S(1)} fusion(s32[]{:T(128)} %bitcast.179, s32[]{:T(128)} %bitcast.178, s32[]{:T(128)} %bitcast.177, s32[]{:T(128)} %bitcast.176, s32[]{:T(128)} %bitcast.175), kind=kLoop, calls=%fused_computation.175 | loop fusion | flops 608 | bytes 148 | tf_op jit(solution)/shard_map/add | solution.py:24
  141.7 2.5 %shift-left_add_fusion.4 = s32[16]{0:T(128)S(1)} fusion(s32[]{:T(128)} %bitcast.196, s32[]{:T(128)} %bitcast.195, s32[]{:T(128)} %bitcast.194, s32[]{:T(128)} %bitcast.193), kind=kLoop, calls=%fused_computation.170 | loop fusion | flops 240 | bytes 80 | tf_op jit(solution)/shard_map/add | solution.py:24
  144.3 3.2 %shift-left_add_fusion.5 = s32[32]{0:T(128)S(1)} fusion(s32[]{:T(128)} %bitcast.192, s32[]{:T(128)} %bitcast.191, s32[]{:T(128)} %bitcast.190, s32[]{:T(128)} %bitcast.189, s32[]{:T(128)} %bitcast.188), kind=kLoop, calls=%fused_computation.171 | loop fusion | flops 608 | bytes 148 | tf_op jit(solution)/shard_map/add | solution.py:24
  172.6 2.5 %gather_fusion.14 = f32[512,2,128]{2,1,0:T(2,128)} fusion(f32[2,512,128]{2,0,1:T(2,128)S(1)} %copy.118, s32[1024]{0:T(1024)S(1)} %get-tuple-element.217), kind=kCustom, calls=%fused_computation.14 | custom fusion | bytes 1050624 | tf_op jit(solution)/shard_map/jit(_take)/gather | solution.py:100
  175.1 3.7 %all-to-all-start.1 = ((f32[2,4,16384]{2,0,1:T(2,128)}), f32[2,4,16384]{2,0,1:T(2,128)S(1)}, u32[]{:S(2)}, u32[]{:S(2)}) async-start(f32[2,4,16384]{2,0,1:T(2,128)} %bitcast.212), calls=%async_computation.1 | async-start | bytes 1048576 | tf_op jit(solution)/shard_map/all_to_all | solution.py:103
  178.8 3.1 %shift-left_add_fusion.1 = s32[32]{0:T(128)S(1)} fusion(s32[]{:T(128)} %bitcast.220, s32[]{:T(128)} %bitcast.219, s32[]{:T(128)} %bitcast.218, s32[]{:T(128)} %bitcast.217, s32[]{:T(128)} %bitcast.216), kind=kLoop, calls=%fused_computation.165 | loop fusion | flops 608 | bytes 148 | tf_op jit(solution)/shard_map/add | solution.py:24
  182.1 5.4 %all-to-all-done.1 = f32[2,4,16384]{2,0,1:T(2,128)S(1)} async-done(((f32[2,4,16384]{2,0,1:T(2,128)}), f32[2,4,16384]{2,0,1:T(2,128)S(1)}, u32[]{:S(2)}, u32[]{:S(2)}) %all-to-all-start.1) | async-done | bytes 524320 | tf_op jit(solution)/shard_map/all_to_all | solution.py:103
  187.5 2.5 %gather_fusion.15 = f32[512,2,128]{2,1,0:T(2,128)} fusion(f32[2,512,128]{2,0,1:T(2,128)S(1)} %bitcast.341, s32[1024]{0:T(1024)S(1)} %pad_clamp_fusion), kind=kCustom, calls=%fused_computation.15 | custom fusion | bytes 1050624 | tf_op jit(solution)/shard_map/jit(_take)/gather | solution.py:104
  (215 shorter events, 110.7 us)
Async XLA Ops:
  0.0 12.2 %copy-start = (f32[1,1,2,65536]{3,2,1,0:T(2,128)S(1)}, f32[1,1,2,65536]{3,2,1,0:T(2,128)}, u32[]{:S(2)}) copy-start(f32[1,1,2,65536]{3,2,1,0:T(2,128)} %param.5) | copy-start | bytes 1572868
  0.0 1.7 copy-start.3
  2.7 0.7 copy-start.4
  14.3 1.0 copy-start.1
  15.3 1.0 copy-start.2
  83.3 68.2 %all-to-all-start = ((f32[8,2,1,8192]{3,2,1,0:T(1,128)}), f32[8,2,1,8192]{3,2,1,0:T(1,128)S(1)}, u32[]{:S(2)}, u32[]{:S(2)}) async-start(f32[8,2,1,8192]{3,2,1,0:T(1,128)} %fusion.48), calls=%async_computation | async-start | bytes 1048576 | tf_op jit(solution)/shard_map/all_to_all | solution.py:9
  175.1 12.4 %all-to-all-start.1 = ((f32[2,4,16384]{2,0,1:T(2,128)}), f32[2,4,16384]{2,0,1:T(2,128)S(1)}, u32[]{:S(2)}, u32[]{:S(2)}) async-start(f32[2,4,16384]{2,0,1:T(2,128)} %bitcast.212), calls=%async_computation.1 | async-start | bytes 1048576 | tf_op jit(solution)/shard_map/all_to_all | solution.py:103
